TPU v7x, 128 devices: a whole 4x4x4 slice. The times are simulated.
128 devices in a mesh: rad: 8 (over y_hi, z), ang: 16 (over x, y_lo, core).
Axes of the slice: x: 4, y: 4 (y_hi: 2, y_lo: 2; y = y_hi * 2 + y_lo), z: 4, core: 2. Of those that a mesh axis runs over, the one named last changes fastest.
Arguments:
- coarse_field: float32 [2, 8, 64, 128], P(None, 'rad', 'ang'), may hold values from -6 to 6
- excite_mid: float32 [2, 8, 8, 64, 128], P(None, None, 'rad', 'ang'), may hold values from -6 to 6
- excite_fine: float32 [2, 8, 16, 128, 256], P(None, None, 'rad', 'ang'), may hold values from -6 to 6
- kernels_mid: float32 [16, 8, 27], replicated, may hold values from -0.875 to 0.875
- noise_mid: float32 [16, 8, 8], replicated, may hold values from -1 to 1
- rows_mid: int32 [8], replicated, may hold values from 0 to 15
- kernels_fine: float32 [16, 8, 27], replicated, may hold values from -0.875 to 0.875
- noise_fine: float32 [16, 8, 8], replicated, may hold values from -1 to 1
- rows_fine: int32 [16], replicated, may hold values from 0 to 15
- emission: float32 [32, 256, 512], P('rad', 'ang'), may hold values from 0.3 to 3
- star_bins: int32 [4, 256, 512], P(None, 'ang'), may hold values from 0 to 31
- star_data: float32 [4, 256, 512], P(None, 'ang'), may hold values from -3 to 3
Outputs:
- grad_coarse: float32 [2, 8, 64, 128], P(None, 'rad', 'ang')
- grad_excite_mid: float32 [2, 8, 8, 64, 128], P(None, None, 'rad', 'ang')
- grad_excite_fine: float32 [2, 8, 16, 128, 256], P(None, None, 'rad', 'ang')
- residual: float32 [2, 4, 256, 512], P(None, None, 'ang')
All inputs are finite; a program needn't handle non-finite values.
Results may differ from a plain program's by a relative error of at most 0.0003.
Values sent between devices are 32-bit elements; how exact they have to be, the bound alone decides.
A program may use at most 192 MiB of HBM per device.

v0:
```python
import jax
import jax.numpy as jnp
from jax import lax
from jax.experimental import pallas as pl
from jax.experimental.pallas import tpu as pltpu
from jax.sharding import PartitionSpec as P

F32 = jnp.float32
BF16 = jnp.bfloat16
MESH = pl.DeviceIdType.MESH
ANY = pl.BlockSpec(memory_space=pl.ANY)
SMEM = pl.BlockSpec(memory_space=pltpu.SMEM)

RING2 = [(di, dk) for di in range(-2, 3) for dk in (-1, 0, 1) if (di, dk) != (0, 0)]
MROWS = [(-1, 1), (0, 0), (0, 1), (1, 0)]


def slot_of(di, dk):
    return (di + 2) * 3 + dk + 1


def lane_shift(x, step):
    if step == 1:
        return x
    width = x.shape[1]
    lane = lax.broadcasted_iota(jnp.int32, x.shape, 1)
    if step == 0:
        return jnp.where(lane == 0, F32(0.0), pltpu.roll(x, 1, 1))
    return jnp.where(lane == width - 1, F32(0.0), pltpu.roll(x, width - 1, 1))


def permuted(x, permutation):
    high = x.astype(BF16)
    rest = x - high.astype(F32)
    mid = rest.astype(BF16)
    low = (rest - mid.astype(F32)).astype(BF16)

    def times(part):
        return jnp.dot(part, permutation, preferred_element_type=F32)

    return times(high) + times(mid) + times(low)


SCRATCH = dict(
    slots=pltpu.VMEM((15, 2, 4, 128), F32),
    exm_v=pltpu.VMEM((2, 8, 4, 128), F32),
    exf_v=pltpu.VMEM((2, 8, 2, 8, 256), F32),
    em_v=pltpu.VMEM((4, 64, 128), F32),
    bins_v=pltpu.VMEM((4, 64, 128), jnp.int32),
    data_v=pltpu.VMEM((4, 64, 128), F32),
    spread_m=pltpu.VMEM((256, 256), BF16),
    gather_m=pltpu.VMEM((256, 256), BF16),
    ne=pltpu.VMEM((4, 4, 2, 4, 128), F32),
    ne_edge=pltpu.VMEM((2, 2, 4, 128), F32),
    ne_side=pltpu.VMEM((2, 4, 4, 128), F32),
    nex=pltpu.VMEM((4, 4, 16, 128), F32),
    ce=pltpu.VMEM((5, 2, 8, 128), F32),
    cs=pltpu.VMEM((5, 9, 16, 128), F32),
    xi=pltpu.VMEM((4, 2, 16, 256), F32),
    f16=pltpu.VMEM((2, 4, 2, 16, 128), F32),
    fs=pltpu.VMEM((4, 9, 16, 256), F32),
    esend=pltpu.VMEM((256, 128), F32),
    erecv=pltpu.VMEM((256, 128), F32),
    dsend=pltpu.VMEM((512, 128), F32),
    drecv=pltpu.VMEM((512, 128), F32),
    gsend=pltpu.VMEM((512, 128), F32),
    grecv=pltpu.VMEM((512, 128), F32),
    colv=pltpu.VMEM((512, 128), F32),
    star_x=pltpu.VMEM((2, 8, 8, 512), F32),
    star_y=pltpu.VMEM((2, 4, 8, 128), F32),
    star_z=pltpu.VMEM((2, 2, 32, 128), F32),
    res_x=pltpu.VMEM((2, 32, 128), F32),
    rsend=pltpu.VMEM((64, 128), F32),
    rrecv=pltpu.VMEM((512, 128), F32),
    res_v=pltpu.VMEM((4, 128, 128), F32),
    gf_v=pltpu.VMEM((2, 8, 2, 8, 256), F32),
    ws=pltpu.VMEM((4, 9, 16, 256), F32),
    g16=pltpu.VMEM((2, 4, 2, 16, 128), F32),
    hh=pltpu.VMEM((4, 2, 16, 256), F32),
    h_edge=pltpu.VMEM((2, 4, 4, 128), F32),
    h_rad=pltpu.VMEM((2, 2, 16, 256), F32),
    h_side=pltpu.VMEM((2, 4, 4, 128), F32),
    wq=pltpu.VMEM((5, 9, 16, 128), F32),
    gcx=pltpu.VMEM((5, 16, 128), F32),
    gslots=pltpu.VMEM((15, 16, 128), F32),
    gm_v=pltpu.VMEM((2, 8, 4, 128), F32),
    gc_v=pltpu.VMEM((2, 4, 128), F32),
    local_sem=pltpu.SemaphoreType.DMA((16,)),
    self_sem=pltpu.SemaphoreType.DMA((8,)),
    out_sem=pltpu.SemaphoreType.DMA((8,)),
    cs_send=pltpu.SemaphoreType.DMA((15,)),
    cs_recv=pltpu.SemaphoreType.DMA((15,)),
    ne_send=pltpu.SemaphoreType.DMA((8,)),
    ne_recv=pltpu.SemaphoreType.DMA((8,)),
    e_send=pltpu.SemaphoreType.DMA((8,)),
    e_recv=pltpu.SemaphoreType.DMA((8,)),
    d_send=pltpu.SemaphoreType.DMA((8,)),
    d_recv=pltpu.SemaphoreType.DMA((8,)),
    g_send=pltpu.SemaphoreType.DMA((8,)),
    g_recv=pltpu.SemaphoreType.DMA((8,)),
    r_send=pltpu.SemaphoreType.DMA((8,)),
    r_recv=pltpu.SemaphoreType.DMA((8,)),
    h_send=pltpu.SemaphoreType.DMA((8,)),
    h_recv=pltpu.SemaphoreType.DMA((8,)),
    q_send=pltpu.SemaphoreType.DMA((15,)),
    q_recv=pltpu.SemaphoreType.DMA((15,)),
)
INPUTS = ["cf", "exm", "exf", "km", "nm", "rm", "kf", "nf", "rf", "emi", "bins", "data"]
OUTPUTS = ["gc_o", "gm_o", "gf_o", "res_o"]


class Refs:
    def __init__(self, refs):
        for name, ref in zip(INPUTS + OUTPUTS + list(SCRATCH), refs):
            setattr(self, name, ref)


def kernel(nr, na, *refs):
    v = Refs(refs)
    i = lax.axis_index("rad")
    k = lax.axis_index("ang")
    coarse_a = 4 * na

    def row_at(di):
        return lax.rem(i + (di + nr), nr)

    def block_at(dk):
        return lax.rem(k + (dk + na), na)

    def remote(src, dst, send, recv, di, dk):
        return pltpu.make_async_remote_copy(
            src_ref=src,
            dst_ref=dst,
            send_sem=send,
            recv_sem=recv,
            device_id=(row_at(di), block_at(dk)),
            device_id_type=MESH,
        )

    def part(ref, index, size):
        return ref.at[pl.ds(pl.multiple_of(index * size, size), size)]

    peers = [(d, 0) for d in range(1, nr)] + [(di, dk) for di, dk in RING2 if dk != 0]
    barrier = pltpu.get_barrier_semaphore()
    for di, dk in peers:
        pl.semaphore_signal(
            barrier, inc=1, device_id=(row_at(di), block_at(dk)), device_id_type=MESH
        )

    loads = [
        pltpu.make_async_copy(v.exm.at[:, :, 0], v.exm_v, v.local_sem.at[0]),
        pltpu.make_async_copy(v.cf.at[:, 0], v.slots.at[slot_of(0, 0)], v.local_sem.at[1]),
    ]
    for c in range(4):
        lanes = pl.ds(128 * c, 128)
        for t, (src, dst) in enumerate(
            ((v.emi, v.em_v), (v.bins, v.bins_v), (v.data, v.data_v))
        ):
            loads.append(
                pltpu.make_async_copy(
                    src.at[:, :, lanes],
                    dst.at[c].reshape(4, 16, 128),
                    v.local_sem.at[2 + 4 * t + c],
                )
            )
    loads.append(pltpu.make_async_copy(v.exf, v.exf_v, v.local_sem.at[14]))
    for load in loads:
        load.start()

    row = lax.broadcasted_iota(jnp.int32, (256, 256), 0)
    col = lax.broadcasted_iota(jnp.int32, (256, 256), 1)
    one, none = F32(1.0), F32(0.0)
    v.gather_m[...] = jnp.where(
        row == 2 * lax.bitwise_and(col, 127) + lax.shift_right_logical(col, 7), one, none
    ).astype(BF16)
    v.spread_m[...] = jnp.where(
        col == 2 * lax.bitwise_and(row, 127) + lax.shift_right_logical(row, 7), one, none
    ).astype(BF16)

    loads[0].wait()
    mid_row = v.rm[i]
    for cr in range(2):
        for q in range(4):
            for s in range(2):
                total = v.nm[mid_row, 4 * cr + q, 0] * v.exm_v[s, 0]
                for j in range(1, 8):
                    total = total + v.nm[mid_row, 4 * cr + q, j] * v.exm_v[s, j]
                v.ne[1 + cr, q, s] = total
                ca, cb = q // 2, q % 2
                if ca == 1:
                    v.ne_edge[0, cr, pl.ds(2 * cb + s, 1)] = total[3:4]
                else:
                    v.ne_edge[1, cr, pl.ds(2 * cb + s, 1)] = total[0:1]
    loads[1].wait()

    pl.semaphore_wait(barrier, len(peers))

    halo = [
        remote(
            v.cf.at[:, 0],
            v.slots.at[slot_of(-di, -dk)],
            v.cs_send.at[slot_of(di, dk)],
            v.cs_recv.at[slot_of(-di, -dk)],
            di,
            dk,
        )
        for di, dk in RING2
    ]
    moves = [(v.ne.at[1], v.ne.at[3], -1, 0), (v.ne.at[2], v.ne.at[0], 1, 0)]
    for side, dk in ((0, 1), (1, -1)):
        moves += [
            (v.ne_edge.at[side], v.ne_side.at[side, 1:3], 0, dk),
            (v.ne_edge.at[side, 0], v.ne_side.at[side, 3], -1, dk),
            (v.ne_edge.at[side, 1], v.ne_side.at[side, 0], 1, dk),
        ]
    halo += [
        remote(src, dst, v.ne_send.at[n], v.ne_recv.at[n], di, dk)
        for n, (src, dst, di, dk) in enumerate(moves)
    ]
    for copy in halo:
        copy.start()

    for c in range(12):
        loads[2 + c].wait()
    pieces = [
        jnp.concatenate(
            [v.em_v[2 * h + e, pl.ds(16 * rl + ca, 8, stride=2), :] for e in range(2)], axis=1
        )
        for rl in range(4)
        for ca in range(2)
        for h in range(2)
    ]
    pieces = permuted(jnp.concatenate(pieces, axis=0), v.gather_m[...])
    for rl in range(4):
        for ca in range(2):
            for h in range(2):
                n = (rl * 2 + ca) * 2 + h
                for cb in range(2):
                    at = h * 16 + rl * 4 + ca * 2 + cb
                    v.esend[pl.ds(at, 8, stride=32), :] = pieces[
                        8 * n : 8 * n + 8, 128 * cb : 128 * cb + 128
                    ]

    def scatter(src, dst, send, recv, size):
        return [
            remote(part(src, row_at(d), size), part(dst, i, size), send.at[d], recv.at[d], d, 0)
            for d in range(1, nr)
        ]

    def keep_own(src, dst, size, sem):
        return pltpu.make_async_copy(part(src, i, size), part(dst, i, size), sem)

    sends_e = scatter(v.esend, v.erecv, v.e_send, v.e_recv, 32)
    own_e = keep_own(v.esend, v.erecv, 32, v.self_sem.at[0])
    own_e.start()
    for copy in sends_e:
        copy.start()

    for n in range(4):
        for ca in range(2):
            for c in range(4):
                at = pl.ds(16 * n + ca, 8, stride=2)
                lanes = pl.ds(128 * c, 128)
                v.star_x[0, :, 2 * n + ca, lanes] = v.bins_v[c, at, :].astype(F32)
                v.star_x[1, :, 2 * n + ca, lanes] = v.data_v[c, at, :]
    for kind in range(2):
        x = v.star_x[kind, i]
        y = permuted(jnp.concatenate([x[:, :256], x[:, 256:]], axis=0), v.gather_m[...])
        for h in range(2):
            for cb in range(2):
                v.star_y[kind, 2 * h + cb] = y[8 * h : 8 * h + 8, 128 * cb : 128 * cb + 128]
        for h in range(2):
            for cb in range(2):
                for ca in range(2):
                    rows = v.star_y[kind, 2 * h + cb, pl.ds(ca, 4, stride=2), :]
                    for s in range(2):
                        v.star_z[kind, h, pl.ds(4 * s + 2 * ca + cb, 4, stride=8), :] = rows

    for copy in halo:
        copy.wait()

    sub8 = lax.broadcasted_iota(jnp.int32, (8, 128), 0)
    sub16 = lax.bitwise_and(lax.broadcasted_iota(jnp.int32, (16, 128), 0), 7)

    def inside(local_a, di):
        there = jnp.where((i + di >= 0) & (i + di < nr), coarse_a, 0)
        a = 4 * k + local_a
        return (a >= 0) & (a < there)

    for q in range(5):
        for s in range(2):
            v.ce[q, s, 2:6] = v.slots[slot_of(q - 2, 0), s]
            v.ce[q, s, 0:2] = v.slots[slot_of(q - 2, -1), s, 2:4]
            v.ce[q, s, 6:8] = v.slots[slot_of(q - 2, 1), s, 0:2]
        here = inside(sub8 - 2, q - 2)
        both = [jnp.where(here, v.ce[q, s], none) for s in range(2)]
        for da in range(3):
            if da == 1:
                moved = both
            else:
                moved = [pltpu.roll(x, 1 if da == 0 else 7, 0) for x in both]
            moved = jnp.concatenate(moved, axis=0)
            for db in range(3):
                v.cs[q, 3 * da + db] = lane_shift(moved, db)

    for m in range(4):
        for q in range(4):
            for s in range(2):
                v.nex[m, q, 8 * s + 2 : 8 * s + 6] = v.ne[m, q, s]
                ca, cb = q // 2, q % 2
                if ca == 1:
                    v.nex[m, q, 8 * s + 1 : 8 * s + 2] = v.ne_side[0, m, pl.ds(2 * cb + s, 1)]
                else:
                    v.nex[m, q, 8 * s + 6 : 8 * s + 7] = v.ne_side[1, m, pl.ds(2 * cb + s, 1)]

    table_row = {}
    for di in (-1, 0, 1):
        table_row[di] = v.rm[jnp.clip(i + di, 0, nr - 1)]
    for m, (di, cr) in enumerate(MROWS):
        sums = [v.nex[m, q] for q in range(4)]
        for o in range(27):
            x = v.cs[di + 1 + o // 9, o % 9]
            for q in range(4):
                sums[q] = sums[q] + v.km[table_row[di], 4 * cr + q, o] * x
        used = inside(sub16 - 2, di) & (sub16 >= 1) & (sub16 <= 6)
        for q in range(4):
            lanes = slice(128 * (q % 2), 128 * (q % 2) + 128)
            v.xi[m, q // 2, :, lanes] = jnp.where(used, sums[q], none)
    spread = permuted(v.xi[...].reshape(128, 256), v.spread_m[...])
    for m in range(4):
        for ca in range(2):
            for s in range(2):
                n = (m * 2 + ca) * 16 + 8 * s
                for h in range(2):
                    v.f16[h, m, s, pl.ds(ca, 8, stride=2), :] = spread[
                        n : n + 8, 128 * h : 128 * h + 128
                    ]
    for m in range(4):
        for da in range(3):
            rows = slice(3 + da, 11 + da)
            x = jnp.concatenate(
                [
                    jnp.concatenate([v.f16[h, m, s, rows, :] for h in range(2)], axis=1)
                    for s in range(2)
                ],
                axis=0,
            )
            for db in range(3):
                v.fs[m, 3 * da + db] = lane_shift(x, db)

    loads[14].wait()
    fine_row = [v.rf[2 * i + r] for r in range(2)]
    for r in range(2):
        for half in range(2):
            sums = [None] * 4
            for j in range(8):
                x = jnp.concatenate([v.exf_v[s, j, r] for s in range(2)], axis=0)
                for q in range(4):
                    term = v.nf[fine_row[r], 4 * half + q, j] * x
                    sums[q] = term if j == 0 else sums[q] + term
            for o in range(27):
                x = v.fs[r + o // 9, o % 9]
                for q in range(4):
                    sums[q] = sums[q] + v.kf[fine_row[r], 4 * half + q, o] * x
            for q in range(4):
                density = jnp.exp(sums[q])
                for s in range(2):
                    for h in range(2):
                        at = h * 32 + (2 * r + half) * 8 + 4 * s + q
                        v.dsend[pl.ds(at, 8, stride=64), :] = density[
                            8 * s : 8 * s + 8, 128 * h : 128 * h + 128
                        ]
    sends_d = scatter(v.dsend, v.drecv, v.d_send, v.d_recv, 64)
    own_d = keep_own(v.dsend, v.drecv, 64, v.self_sem.at[1])
    for copy in sends_d:
        copy.start()
    own_d.start()

    for copy in sends_e:
        copy.wait()
    own_e.wait()
    for copy in sends_d:
        copy.wait()
    own_d.wait()

    spacing = F32(1.0 / (4 * nr))
    cells = 4 * nr
    for h in range(2):
        bins = [v.star_z[0, h, 8 * n : 8 * n + 8] for n in range(4)]
        seen = [v.star_z[1, h, 8 * n : 8 * n + 8] for n in range(4)]
        depth = jnp.zeros((8, 128), F32)
        column = jnp.zeros((8, 128), F32)
        picked = [jnp.zeros((8, 128), F32) for _ in range(4)]
        for cell in range(cells):
            at = (cell // 4) * 64 + h * 32 + (cell % 4) * 8
            ea = (cell // 4) * 32 + h * 16 + (cell % 4) * 4
            light = v.erecv[ea : ea + 4]
            light = jnp.concatenate([light, light], axis=0)
            column = column + spacing * light * jnp.exp(-depth)
            depth = depth + spacing * v.drecv[at : at + 8]
            v.colv[at : at + 8] = column
            for n in range(4):
                picked[n] = jnp.where(bins[n] == F32(cell), column, picked[n])
        left = [seen[n] - picked[n] for n in range(4)]
        for n in range(4):
            v.res_x[h, 8 * n : 8 * n + 8] = left[n]
        for cell in range(cells):
            at = (cell // 4) * 64 + h * 32 + (cell % 4) * 8
            column = v.colv[at : at + 8]
            weight = None
            for n in range(4):
                term = jnp.where(
                    bins[n] > F32(cell), left[n] * (picked[n] - column), F32(0.0)
                )
                weight = term if n == 0 else weight + term
            v.gsend[at : at + 8] = -v.drecv[at : at + 8] * weight
    sends_g = scatter(v.gsend, v.grecv, v.g_send, v.g_recv, 64)
    own_g = keep_own(v.gsend, v.grecv, 64, v.self_sem.at[2])
    for copy in sends_g:
        copy.start()
    own_g.start()

    pieces = [
        jnp.concatenate([v.res_x[h, pl.ds(cb, 16, stride=2), :] for cb in range(2)], axis=1)
        for h in range(2)
    ]
    spread = permuted(jnp.concatenate(pieces, axis=0), v.spread_m[...])
    for h in range(2):
        for e in range(2):
            c = 2 * h + e
            v.rsend[16 * c : 16 * c + 16] = spread[
                16 * h : 16 * h + 16, 128 * e : 128 * e + 128
            ]
    sends_r = [
        remote(v.rsend, part(v.rrecv, i, 64), v.r_send.at[d], v.r_recv.at[d], d, 0)
        for d in range(1, nr)
    ]
    own_r = pltpu.make_async_copy(v.rsend, part(v.rrecv, i, 64), v.self_sem.at[3])
    for copy in sends_r:
        copy.start()
    own_r.start()

    for copy in sends_g:
        copy.wait()
    own_g.wait()

    for r in range(2):
        grads = []
        for c in range(8):
            cr, q = c // 4, c % 4
            at = [[h * 32 + (2 * r + cr) * 8 + 4 * s + q for h in range(2)] for s in range(2)]
            grads.append(
                jnp.concatenate(
                    [
                        jnp.concatenate(
                            [v.grecv[pl.ds(at[s][h], 8, stride=64), :] for h in range(2)], axis=1
                        )
                        for s in range(2)
                    ],
                    axis=0,
                )
            )
        for j in range(8):
            total = v.nf[fine_row[r], 0, j] * grads[0]
            for c in range(1, 8):
                total = total + v.nf[fine_row[r], c, j] * grads[c]
            for s in range(2):
                v.gf_v[s, j, r] = total[8 * s : 8 * s + 8]
        for o in range(27):
            total = v.kf[fine_row[r], 0, o] * grads[0]
            for c in range(1, 8):
                total = total + v.kf[fine_row[r], c, o] * grads[c]
            m = r + o // 9
            if r == 1 and m < 3:
                total = total + v.ws[m, o % 9]
            v.ws[m, o % 9] = total
    out_gf = pltpu.make_async_copy(v.gf_v, v.gf_o, v.out_sem.at[0])
    out_gf.start()

    v.g16[...] = jnp.zeros(v.g16.shape, F32)
    for m in range(4):
        for da in range(3):
            total = lane_shift(v.ws[m, 3 * da + 1], 1)
            total = total + lane_shift(v.ws[m, 3 * da], 2)
            total = total + lane_shift(v.ws[m, 3 * da + 2], 0)
            rows = slice(3 + da, 11 + da)
            for h in range(2):
                for s in range(2):
                    v.g16[h, m, s, rows, :] = (
                        v.g16[h, m, s, rows, :]
                        + total[8 * s : 8 * s + 8, 128 * h : 128 * h + 128]
                    )
    pieces = []
    for m in range(4):
        here = inside(sub8 - 2, MROWS[m][0])
        for ca in range(2):
            for s in range(2):
                pieces.append(
                    jnp.concatenate(
                        [
                            jnp.where(here, v.g16[h, m, s, pl.ds(ca, 8, stride=2), :], none)
                            for h in range(2)
                        ],
                        axis=1,
                    )
                )
    v.hh[...] = permuted(jnp.concatenate(pieces, axis=0), v.gather_m[...]).reshape(4, 2, 16, 256)
    for m in range(4):
        for s in range(2):
            for cb in range(2):
                lanes = slice(128 * cb, 128 * cb + 128)
                v.h_edge[0, m, pl.ds(2 * s + cb, 1)] = v.hh[m, 1, 8 * s + 1 : 8 * s + 2, lanes]
                v.h_edge[1, m, pl.ds(2 * s + cb, 1)] = v.hh[m, 0, 8 * s + 6 : 8 * s + 7, lanes]
    moves = [(v.hh.at[0], v.h_rad.at[1], -1, 0), (v.hh.at[3], v.h_rad.at[0], 1, 0)]
    for side, dk in ((0, -1), (1, 1)):
        moves += [
            (v.h_edge.at[side, 1:3], v.h_side.at[side, 0:2], 0, dk),
            (v.h_edge.at[side, 0], v.h_side.at[side, 3], -1, dk),
            (v.h_edge.at[side, 3], v.h_side.at[side, 2], 1, dk),
        ]
    owed = [
        remote(src, dst, v.h_send.at[n], v.h_recv.at[n], di, dk)
        for n, (src, dst, di, dk) in enumerate(moves)
    ]
    for copy in owed:
        copy.start()

    for di in (-1, 0, 1):
        children = []
        for m, (mdi, cr) in enumerate(MROWS):
            if mdi == di:
                for q in range(4):
                    lanes = slice(128 * (q % 2), 128 * (q % 2) + 128)
                    children.append((4 * cr + q, v.hh[m, q // 2, :, lanes]))
        for o in range(27):
            total = None
            for c, x in children:
                term = v.km[table_row[di], c, o] * x
                total = term if total is None else total + term
            row_q = di + 1 + o // 9
            if di > -1 and row_q < di + 3:
                total = total + v.wq[row_q, o % 9]
            v.wq[row_q, o % 9] = total
    for q in range(5):
        pieces = []
        for da in range(3):
            total = v.wq[q, 3 * da + 1]
            total = total + lane_shift(v.wq[q, 3 * da], 2)
            total = total + lane_shift(v.wq[q, 3 * da + 2], 0)
            pieces.append(total)
        here = inside(sub8 - 2, q - 2)
        for s in range(2):
            rows = slice(8 * s, 8 * s + 8)
            total = pieces[1][rows]
            total = total + pltpu.roll(pieces[0][rows], 7, 0)
            total = total + pltpu.roll(pieces[2][rows], 1, 0)
            v.gcx[q, rows] = jnp.where(here, total, none)
    owed_q = [
        remote(
            v.gcx.at[di + 2],
            v.gslots.at[slot_of(-di, -dk)],
            v.q_send.at[slot_of(di, dk)],
            v.q_recv.at[slot_of(-di, -dk)],
            di,
            dk,
        )
        for di, dk in RING2
    ]
    for copy in owed_q:
        copy.start()

    for copy in sends_r:
        copy.wait()
    own_r.wait()
    for c in range(4):
        for n in range(4):
            for s in range(2):
                for ca in range(2):
                    at = 16 * c + n * 4 + s * 2 + ca
                    v.res_v[c, pl.ds((s * 4 + n) * 16 + ca, 8, stride=2), :] = v.rrecv[
                        pl.ds(at, 8, stride=64), :
                    ]
    outs = [
        pltpu.make_async_copy(
            v.res_v.at[c].reshape(2, 4, 16, 128),
            v.res_o.at[:, :, :, pl.ds(128 * c, 128)],
            v.out_sem.at[1 + c],
        )
        for c in range(4)
    ]
    for out in outs:
        out.start()

    for copy in owed:
        copy.wait()
    for s in range(2):
        grads = []
        for cr in range(2):
            for q in range(4):
                ca, cb = q // 2, q % 2
                lanes = slice(128 * cb, 128 * cb + 128)
                rows = slice(8 * s + 2, 8 * s + 6)
                total = v.hh[1 + cr, ca, rows, lanes] + v.h_rad[cr, ca, rows, lanes]
                side, place = (0, 3) if ca == 1 else (1, 0)
                edge = pl.ds(2 * s + cb, 1)
                extra = v.h_side[side, cr, edge] + v.h_side[side, 2 + cr, edge]
                at = lax.broadcasted_iota(jnp.int32, (4, 128), 0)
                grads.append(
                    total + jnp.where(at == place, jnp.broadcast_to(extra, (4, 128)), none)
                )
        for j in range(8):
            total = v.nm[mid_row, 0, j] * grads[0]
            for c in range(1, 8):
                total = total + v.nm[mid_row, c, j] * grads[c]
            v.gm_v[s, j] = total
    out_gm = pltpu.make_async_copy(v.gm_v, v.gm_o.at[:, :, 0], v.out_sem.at[5])
    out_gm.start()

    for copy in owed_q:
        copy.wait()
    for s in range(2):
        total = v.gcx[2, 8 * s + 2 : 8 * s + 6]
        low = jnp.zeros((2, 128), F32)
        high = jnp.zeros((2, 128), F32)
        for di in range(-2, 3):
            if di != 0:
                total = total + v.gslots[slot_of(di, 0), 8 * s + 2 : 8 * s + 6]
            low = low + v.gslots[slot_of(di, -1), 8 * s + 6 : 8 * s + 8]
            high = high + v.gslots[slot_of(di, 1), 8 * s : 8 * s + 2]
        v.gc_v[s] = total + jnp.concatenate([low, high], axis=0)
    out_gc = pltpu.make_async_copy(v.gc_v, v.gc_o.at[:, 0], v.out_sem.at[6])
    out_gc.start()
    for out in [out_gf, *outs, out_gm, out_gc]:
        out.wait()


def per_device(*args):
    import functools

    nr, na = lax.axis_size("rad"), lax.axis_size("ang")
    shapes = [(2, 1, 4, 128), (2, 8, 1, 4, 128), (2, 8, 2, 8, 256), (2, 4, 16, 512)]
    return pl.pallas_call(
        functools.partial(kernel, nr, na),
        out_shape=[jax.ShapeDtypeStruct(shape, F32) for shape in shapes],
        in_specs=[ANY, ANY, ANY] + [SMEM] * 6 + [ANY] * 3,
        out_specs=[ANY] * 4,
        scratch_shapes=list(SCRATCH.values()),
        compiler_params=pltpu.CompilerParams(collective_id=0, has_side_effects=True),
    )(*args)


def solution(mesh):
    placed = (
        P(None, "rad", "ang", None),
        P(None, None, "rad", "ang", None),
        P(None, None, "rad", "ang", None),
        P(),
        P(),
        P(),
        P(),
        P(),
        P(),
        P("rad", "ang", None),
        P(None, "ang", None),
        P(None, "ang", None),
    )
    return jax.shard_map(
        per_device,
        mesh=mesh,
        in_specs=placed,
        out_specs=(
            P(None, "rad", "ang", None),
            P(None, None, "rad", "ang", None),
            P(None, None, "rad", "ang", None),
            P(None, None, "ang", None),
        ),
        check_vma=False,
    )
```

profile of v0, /device:TPU:1, one launch (start us, length us, event | category | flops | bytes accessed | tf_op | source)
XLA Modules:
  0.0 50.4 jit_solution(6546283955167146493)
XLA Ops:
  0.6 0.0 copy-start.1
  0.6 1.5 %copy.16.refs_4_ = f32[16,8,8]{2,1,0:T(8,128)} copy(f32[16,8,8]{0,2,1:T(8,128)} %param.16) | data formatting | bytes 8192 | tf_op args[4]
  2.1 0.0 copy-done.1
  2.1 0.7 %copy.17.refs_7_ = f32[16,8,8]{2,1,0:T(8,128)} copy(f32[16,8,8]{0,2,1:T(8,128)S(1)} %copy-done.1) | data formatting | bytes 8192 | tf_op args[7]
  2.8 42.5 %shard_map.147 = (f32[2,1,4,128]{3,2,1,0:T(4,128)}, f32[2,8,1,4,128]{4,3,2,1,0:T(4,128)}, f32[2,8,2,8,256]{4,3,2,1,0:T(8,128)}, f32[2,4,16,512]{3,2,1,0:T(8,128)}) custom-call(f32[2,1,4,128]{3,2,1,0:T(4,128)} %refs_0_.1, f32[2,8,1,4,128]{4,3,2,1,0:T(4,128)} %refs_1_.1, f32[2,8,2,8,256]{4,3,2,1,0:T(8,128)} %refs_2_.1, f32[16,8,27]{2,1,0:T(8,128)} %refs_3_.1, ...), custom_call_target="tpu_custom_call" | custom-call | tf_op jit(solution)/shard_map/pallas_call | solution.py:642
  45.3 0.0 copy-start.2
  45.3 0.7 %copy-done.2 = f32[2,1,4,128]{3,2,1,0:T(4,128)S(1)} copy-done((f32[2,1,4,128]{3,2,1,0:T(4,128)S(1)}, f32[2,1,4,128]{3,2,1,0:T(4,128)}, u32[]{:S(2)}) %copy-start.2) | copy-done | bytes 4120
  46.0 0.6 %copy.22 = f32[2,1,4,128]{3,2,1,0:T(4,128)} copy(f32[2,1,4,128]{3,2,1,0:T(4,128)S(1)} %copy-done.2) | data formatting | bytes 8192
  46.6 1.4 %copy.23 = f32[2,8,1,4,128]{4,3,2,1,0:T(4,128)} copy(f32[2,8,1,4,128]{4,3,2,1,0:T(4,128)} %get-tuple-element.9) | data formatting | bytes 65536
  48.0 0.0 copy-start
  48.0 1.7 %copy.24 = f32[2,8,2,8,256]{4,3,2,1,0:T(8,128)} copy(f32[2,8,2,8,256]{4,3,2,1,0:T(8,128)} %get-tuple-element.10) | data formatting | bytes 524288
  49.7 0.0 copy-done
  49.7 0.7 %copy.25 = f32[2,4,16,512]{3,2,1,0:T(8,128)} copy(f32[2,4,16,512]{3,2,1,0:T(8,128)S(1)} %copy-done) | data formatting | bytes 524288
Async XLA Ops:
  0.6 1.5 %copy-start.1 = (f32[16,8,8]{0,2,1:T(8,128)S(1)}, f32[16,8,8]{0,2,1:T(8,128)}, u32[]{:S(2)}) copy-start(f32[16,8,8]{0,2,1:T(8,128)} %param.19) | copy-start | bytes 12292
  45.3 0.7 %copy-start.2 = (f32[2,1,4,128]{3,2,1,0:T(4,128)S(1)}, f32[2,1,4,128]{3,2,1,0:T(4,128)}, u32[]{:S(2)}) copy-start(f32[2,1,4,128]{3,2,1,0:T(4,128)} %get-tuple-element.8) | copy-start | bytes 12292
  48.0 1.7 %copy-start = (f32[2,4,16,512]{3,2,1,0:T(8,128)S(1)}, f32[2,4,16,512]{3,2,1,0:T(8,128)}, u32[]{:S(2)}) copy-start(f32[2,4,16,512]{3,2,1,0:T(8,128)} %get-tuple-element.11) | copy-start | bytes 786436
where the time goes:
time: 50.8 us; the launch traced here: 50.4 us
  Pallas kernels  42.5 us (84%)
  local copies, waits for them, and re-layouts  7.24 us (14%)
  between operations  0.66 us (1%)
    pallas_call x1, Pallas kernels, per_device(): pl.pallas_call(functools.partial(kernel, nr, na), out_shape=[jax.ShapeDty...  42.5 us
    unnamed x12, local copies, waits for them, and re-layouts  7.24 us

commit v1 on v0

--- a/solution.py
+++ b/solution.py
@@ -1,3 +1,5 @@
+import functools
+
 import jax
 import jax.numpy as jnp
 from jax import lax
@@ -9,7 +11,7 @@
 BF16 = jnp.bfloat16
 MESH = pl.DeviceIdType.MESH
 ANY = pl.BlockSpec(memory_space=pl.ANY)
-SMEM = pl.BlockSpec(memory_space=pltpu.SMEM)
+VMEM = pl.BlockSpec(memory_space=pltpu.VMEM)
 
 RING2 = [(di, dk) for di in range(-2, 3) for dk in (-1, 0, 1) if (di, dk) != (0, 0)]
 MROWS = [(-1, 1), (0, 0), (0, 1), (1, 0)]
@@ -72,8 +74,6 @@
     res_x=pltpu.VMEM((2, 32, 128), F32),
     rsend=pltpu.VMEM((64, 128), F32),
     rrecv=pltpu.VMEM((512, 128), F32),
-    res_v=pltpu.VMEM((4, 128, 128), F32),
-    gf_v=pltpu.VMEM((2, 8, 2, 8, 256), F32),
     ws=pltpu.VMEM((4, 9, 16, 256), F32),
     g16=pltpu.VMEM((2, 4, 2, 16, 128), F32),
     hh=pltpu.VMEM((4, 2, 16, 256), F32),
@@ -83,11 +83,15 @@
     wq=pltpu.VMEM((5, 9, 16, 128), F32),
     gcx=pltpu.VMEM((5, 16, 128), F32),
     gslots=pltpu.VMEM((15, 16, 128), F32),
-    gm_v=pltpu.VMEM((2, 8, 4, 128), F32),
-    gc_v=pltpu.VMEM((2, 4, 128), F32),
+    km_s=pltpu.SMEM((16, 8, 27), F32),
+    nm_s=pltpu.SMEM((8, 8, 16), F32),
+    kf_s=pltpu.SMEM((16, 8, 27), F32),
+    nf_s=pltpu.SMEM((8, 8, 16), F32),
+    rm_s=pltpu.SMEM((8,), jnp.int32),
+    rf_s=pltpu.SMEM((16,), jnp.int32),
+    table_sem=pltpu.SemaphoreType.DMA((6,)),
     local_sem=pltpu.SemaphoreType.DMA((16,)),
     self_sem=pltpu.SemaphoreType.DMA((8,)),
-    out_sem=pltpu.SemaphoreType.DMA((8,)),
     cs_send=pltpu.SemaphoreType.DMA((15,)),
     cs_recv=pltpu.SemaphoreType.DMA((15,)),
     ne_send=pltpu.SemaphoreType.DMA((8,)),
@@ -106,7 +110,7 @@
     q_recv=pltpu.SemaphoreType.DMA((15,)),
 )
 INPUTS = ["cf", "exm", "exf", "km", "nm", "rm", "kf", "nf", "rf", "emi", "bins", "data"]
-OUTPUTS = ["gc_o", "gm_o", "gf_o", "res_o"]
+OUTPUTS = ["gc_v", "gm_v", "gf_v", "res_v"]
 
 
 class Refs:
@@ -164,7 +168,20 @@
                 )
             )
     loads.append(pltpu.make_async_copy(v.exf, v.exf_v, v.local_sem.at[14]))
-    for load in loads:
+    tables = [
+        pltpu.make_async_copy(src, dst, v.table_sem.at[n])
+        for n, (src, dst) in enumerate(
+            (
+                (v.rm, v.rm_s),
+                (v.nm, v.nm_s),
+                (v.rf, v.rf_s),
+                (v.km, v.km_s),
+                (v.nf, v.nf_s),
+                (v.kf, v.kf_s),
+            )
+        )
+    ]
+    for load in loads[:2] + tables + loads[2:]:
         load.start()
 
     row = lax.broadcasted_iota(jnp.int32, (256, 256), 0)
@@ -178,13 +195,15 @@
     ).astype(BF16)
 
     loads[0].wait()
-    mid_row = v.rm[i]
+    for table in tables:
+        table.wait()
+    mid_row = v.rm_s[i]
     for cr in range(2):
         for q in range(4):
             for s in range(2):
-                total = v.nm[mid_row, 4 * cr + q, 0] * v.exm_v[s, 0]
+                total = v.nm_s[4 * cr + q, 0, mid_row] * v.exm_v[s, 0]
                 for j in range(1, 8):
-                    total = total + v.nm[mid_row, 4 * cr + q, j] * v.exm_v[s, j]
+                    total = total + v.nm_s[4 * cr + q, j, mid_row] * v.exm_v[s, j]
                 v.ne[1 + cr, q, s] = total
                 ca, cb = q // 2, q % 2
                 if ca == 1:
@@ -192,33 +211,6 @@
                 else:
                     v.ne_edge[1, cr, pl.ds(2 * cb + s, 1)] = total[0:1]
     loads[1].wait()
-
-    pl.semaphore_wait(barrier, len(peers))
-
-    halo = [
-        remote(
-            v.cf.at[:, 0],
-            v.slots.at[slot_of(-di, -dk)],
-            v.cs_send.at[slot_of(di, dk)],
-            v.cs_recv.at[slot_of(-di, -dk)],
-            di,
-            dk,
-        )
-        for di, dk in RING2
-    ]
-    moves = [(v.ne.at[1], v.ne.at[3], -1, 0), (v.ne.at[2], v.ne.at[0], 1, 0)]
-    for side, dk in ((0, 1), (1, -1)):
-        moves += [
-            (v.ne_edge.at[side], v.ne_side.at[side, 1:3], 0, dk),
-            (v.ne_edge.at[side, 0], v.ne_side.at[side, 3], -1, dk),
-            (v.ne_edge.at[side, 1], v.ne_side.at[side, 0], 1, dk),
-        ]
-    halo += [
-        remote(src, dst, v.ne_send.at[n], v.ne_recv.at[n], di, dk)
-        for n, (src, dst, di, dk) in enumerate(moves)
-    ]
-    for copy in halo:
-        copy.start()
 
     for c in range(12):
         loads[2 + c].wait()
@@ -249,12 +241,6 @@
 
     def keep_own(src, dst, size, sem):
         return pltpu.make_async_copy(part(src, i, size), part(dst, i, size), sem)
-
-    sends_e = scatter(v.esend, v.erecv, v.e_send, v.e_recv, 32)
-    own_e = keep_own(v.esend, v.erecv, 32, v.self_sem.at[0])
-    own_e.start()
-    for copy in sends_e:
-        copy.start()
 
     for n in range(4):
         for ca in range(2):
@@ -276,6 +262,39 @@
                     for s in range(2):
                         v.star_z[kind, h, pl.ds(4 * s + 2 * ca + cb, 4, stride=8), :] = rows
 
+    pl.semaphore_wait(barrier, len(peers))
+
+    halo = [
+        remote(
+            v.cf.at[:, 0],
+            v.slots.at[slot_of(-di, -dk)],
+            v.cs_send.at[slot_of(di, dk)],
+            v.cs_recv.at[slot_of(-di, -dk)],
+            di,
+            dk,
+        )
+        for di, dk in RING2
+    ]
+    moves = [(v.ne.at[1], v.ne.at[3], -1, 0), (v.ne.at[2], v.ne.at[0], 1, 0)]
+    for side, dk in ((0, 1), (1, -1)):
+        moves += [
+            (v.ne_edge.at[side], v.ne_side.at[side, 1:3], 0, dk),
+            (v.ne_edge.at[side, 0], v.ne_side.at[side, 3], -1, dk),
+            (v.ne_edge.at[side, 1], v.ne_side.at[side, 0], 1, dk),
+        ]
+    halo += [
+        remote(src, dst, v.ne_send.at[n], v.ne_recv.at[n], di, dk)
+        for n, (src, dst, di, dk) in enumerate(moves)
+    ]
+    for copy in halo:
+        copy.start()
+
+    sends_e = scatter(v.esend, v.erecv, v.e_send, v.e_recv, 32)
+    own_e = keep_own(v.esend, v.erecv, 32, v.self_sem.at[0])
+    own_e.start()
+    for copy in sends_e:
+        copy.start()
+
     for copy in halo:
         copy.wait()
 
@@ -315,13 +334,13 @@
 
     table_row = {}
     for di in (-1, 0, 1):
-        table_row[di] = v.rm[jnp.clip(i + di, 0, nr - 1)]
+        table_row[di] = v.rm_s[jnp.clip(i + di, 0, nr - 1)]
     for m, (di, cr) in enumerate(MROWS):
         sums = [v.nex[m, q] for q in range(4)]
         for o in range(27):
             x = v.cs[di + 1 + o // 9, o % 9]
             for q in range(4):
-                sums[q] = sums[q] + v.km[table_row[di], 4 * cr + q, o] * x
+                sums[q] = sums[q] + v.km_s[table_row[di], 4 * cr + q, o] * x
         used = inside(sub16 - 2, di) & (sub16 >= 1) & (sub16 <= 6)
         for q in range(4):
             lanes = slice(128 * (q % 2), 128 * (q % 2) + 128)
@@ -349,19 +368,19 @@
                 v.fs[m, 3 * da + db] = lane_shift(x, db)
 
     loads[14].wait()
-    fine_row = [v.rf[2 * i + r] for r in range(2)]
+    fine_row = [v.rf_s[2 * i + r] for r in range(2)]
     for r in range(2):
         for half in range(2):
             sums = [None] * 4
             for j in range(8):
                 x = jnp.concatenate([v.exf_v[s, j, r] for s in range(2)], axis=0)
                 for q in range(4):
-                    term = v.nf[fine_row[r], 4 * half + q, j] * x
+                    term = v.nf_s[4 * half + q, j, fine_row[r]] * x
                     sums[q] = term if j == 0 else sums[q] + term
             for o in range(27):
                 x = v.fs[r + o // 9, o % 9]
                 for q in range(4):
-                    sums[q] = sums[q] + v.kf[fine_row[r], 4 * half + q, o] * x
+                    sums[q] = sums[q] + v.kf_s[fine_row[r], 4 * half + q, o] * x
             for q in range(4):
                 density = jnp.exp(sums[q])
                 for s in range(2):
@@ -461,22 +480,19 @@
                 )
             )
         for j in range(8):
-            total = v.nf[fine_row[r], 0, j] * grads[0]
+            total = v.nf_s[0, j, fine_row[r]] * grads[0]
             for c in range(1, 8):
-                total = total + v.nf[fine_row[r], c, j] * grads[c]
+                total = total + v.nf_s[c, j, fine_row[r]] * grads[c]
             for s in range(2):
                 v.gf_v[s, j, r] = total[8 * s : 8 * s + 8]
         for o in range(27):
-            total = v.kf[fine_row[r], 0, o] * grads[0]
+            total = v.kf_s[fine_row[r], 0, o] * grads[0]
             for c in range(1, 8):
-                total = total + v.kf[fine_row[r], c, o] * grads[c]
+                total = total + v.kf_s[fine_row[r], c, o] * grads[c]
             m = r + o // 9
             if r == 1 and m < 3:
                 total = total + v.ws[m, o % 9]
             v.ws[m, o % 9] = total
-    out_gf = pltpu.make_async_copy(v.gf_v, v.gf_o, v.out_sem.at[0])
-    out_gf.start()
-
     v.g16[...] = jnp.zeros(v.g16.shape, F32)
     for m in range(4):
         for da in range(3):
@@ -535,7 +551,7 @@
         for o in range(27):
             total = None
             for c, x in children:
-                term = v.km[table_row[di], c, o] * x
+                term = v.km_s[table_row[di], c, o] * x
                 total = term if total is None else total + term
             row_q = di + 1 + o // 9
             if di > -1 and row_q < di + 3:
@@ -580,17 +596,6 @@
                     v.res_v[c, pl.ds((s * 4 + n) * 16 + ca, 8, stride=2), :] = v.rrecv[
                         pl.ds(at, 8, stride=64), :
                     ]
-    outs = [
-        pltpu.make_async_copy(
-            v.res_v.at[c].reshape(2, 4, 16, 128),
-            v.res_o.at[:, :, :, pl.ds(128 * c, 128)],
-            v.out_sem.at[1 + c],
-        )
-        for c in range(4)
-    ]
-    for out in outs:
-        out.start()
-
     for copy in owed:
         copy.wait()
     for s in range(2):
@@ -609,13 +614,10 @@
                     total + jnp.where(at == place, jnp.broadcast_to(extra, (4, 128)), none)
                 )
         for j in range(8):
-            total = v.nm[mid_row, 0, j] * grads[0]
+            total = v.nm_s[0, j, mid_row] * grads[0]
             for c in range(1, 8):
-                total = total + v.nm[mid_row, c, j] * grads[c]
+                total = total + v.nm_s[c, j, mid_row] * grads[c]
             v.gm_v[s, j] = total
-    out_gm = pltpu.make_async_copy(v.gm_v, v.gm_o.at[:, :, 0], v.out_sem.at[5])
-    out_gm.start()
-
     for copy in owed_q:
         copy.wait()
     for s in range(2):
@@ -628,25 +630,51 @@
             low = low + v.gslots[slot_of(di, -1), 8 * s + 6 : 8 * s + 8]
             high = high + v.gslots[slot_of(di, 1), 8 * s : 8 * s + 2]
         v.gc_v[s] = total + jnp.concatenate([low, high], axis=0)
-    out_gc = pltpu.make_async_copy(v.gc_v, v.gc_o.at[:, 0], v.out_sem.at[6])
-    out_gc.start()
-    for out in [out_gf, *outs, out_gm, out_gc]:
+
+
+def hand_out(gc_v, gm_v, gf_v, res_v, gc_o, gm_o, gf_o, res_o, sem):
+    outs = [
+        pltpu.make_async_copy(gf_v, gf_o, sem.at[0]),
+        pltpu.make_async_copy(gm_v, gm_o.at[:, :, 0], sem.at[1]),
+        pltpu.make_async_copy(gc_v, gc_o.at[:, 0], sem.at[2]),
+    ]
+    for c in range(4):
+        outs.append(
+            pltpu.make_async_copy(
+                res_v.at[c].reshape(2, 4, 16, 128),
+                res_o.at[:, :, :, pl.ds(128 * c, 128)],
+                sem.at[3 + c],
+            )
+        )
+    for out in outs:
+        out.start()
+    for out in outs:
         out.wait()
 
 
 def per_device(*args):
-    import functools
-
     nr, na = lax.axis_size("rad"), lax.axis_size("ang")
+    args = list(args)
+    for n in (4, 7):
+        args[n] = args[n].transpose(1, 2, 0)
+    held = [(2, 4, 128), (2, 8, 4, 128), (2, 8, 2, 8, 256), (4, 128, 128)]
     shapes = [(2, 1, 4, 128), (2, 8, 1, 4, 128), (2, 8, 2, 8, 256), (2, 4, 16, 512)]
-    return pl.pallas_call(
+    results = pl.pallas_call(
         functools.partial(kernel, nr, na),
-        out_shape=[jax.ShapeDtypeStruct(shape, F32) for shape in shapes],
-        in_specs=[ANY, ANY, ANY] + [SMEM] * 6 + [ANY] * 3,
-        out_specs=[ANY] * 4,
+        out_shape=[pltpu.VMEM(shape, F32) for shape in held],
+        in_specs=[ANY] * 12,
+        out_specs=[VMEM] * 4,
         scratch_shapes=list(SCRATCH.values()),
         compiler_params=pltpu.CompilerParams(collective_id=0, has_side_effects=True),
     )(*args)
+    return pl.pallas_call(
+        hand_out,
+        out_shape=[jax.ShapeDtypeStruct(shape, F32) for shape in shapes],
+        in_specs=[VMEM] * 4,
+        out_specs=[ANY] * 4,
+        scratch_shapes=[pltpu.SemaphoreType.DMA((7,))],
+        compiler_params=pltpu.CompilerParams(vmem_limit_bytes=4 << 20),
+    )(*results)
 
 
 def solution(mesh):

time: 50.8 us -> 39 us (0.77)
  local copies, waits for them, and re-layouts: 7.24 us -> 0 us
  Pallas kernels: 42.5 us -> 38.2 us
    unnamed x12 -> x0, local copies, waits for them, and re-layouts: 7.24 us -> none
    pallas_call x1 -> x2, Pallas kernels: 42.5 us -> 38.2 us  [the longest x1 37.3 us: per_device(): pl.pallas_call(functools.partial(kernel, nr, na), out_shape=[pltpu.VMEM(s...]
where the time goes in v1:
time: 39 us; the launch traced here: 38.8 us
  Pallas kernels  38.2 us (98%)
  between operations  0.64 us (2%)
    pallas_call x1, Pallas kernels, per_device(): pl.pallas_call(functools.partial(kernel, nr, na), out_shape=[pltpu.VMEM(s...  37.3 us
    pallas_call x1, Pallas kernels, per_device(): pl.pallas_call(hand_out, out_shape=[jax.ShapeDtypeStruct(shape, F32) for...  0.86 us

profile of v1, /device:TPU:1, one launch (start us, length us, event | category | flops | bytes accessed | tf_op | source)
XLA Modules:
  0.0 38.8 jit_solution(13440505554511434597)
XLA Ops:
  0.6 37.3 %shard_map.147 = (f32[2,4,128]{2,1,0:T(4,128)S(1)}, f32[2,8,4,128]{3,2,1,0:T(4,128)S(1)}, f32[2,8,2,8,256]{4,3,2,1,0:T(8,128)S(1)}, f32[4,128,128]{2,1,0:T(8,128)S(1)}) custom-call(f32[2,1,4,128]{3,2,1,0:T(4,128)} %refs_0_.1, f32[2,8,1,4,128]{4,3,2,1,0:T(4,128)} %refs_1_.1, f32[2,8,2,8,256]{4,3,2,1,0:T(8,128)} %refs_2_.1, f32[16,8,27]{2,1,0:T(8,128)} %refs_3_.1, ...), custom_call_target="tpu_custom_call" | custom-call | tf_op jit(solution)/shard_map/pallas_call | solution.py:662
  38.0 0.9 %shard_map.148 = (f32[2,1,4,128]{3,2,1,0:T(4,128)}, f32[2,8,1,4,128]{4,3,2,1,0:T(4,128)}, f32[2,8,2,8,256]{4,3,2,1,0:T(8,128)}, f32[2,4,16,512]{3,2,1,0:T(8,128)}) custom-call(f32[2,4,128]{2,1,0:T(4,128)S(1)} %get-tuple-element.8.gc_v, f32[2,8,4,128]{3,2,1,0:T(4,128)S(1)} %get-tuple-element.9.gm_v, f32[2,8,2,8,256]{4,3,2,1,0:T(8,128)S(1)} %get-tuple-element.10.gf_v, ...), custom_call_target="tpu_custom_call" | custom-call | tf_op jit(solution)/shard_map/pallas_call | solution.py:670
